TPU v7x, 1024 devices: a whole 4x8x16 slice. The times are simulated.
1024 devices in a mesh: section: 16 (over y, core), expert: 64 (over z, x).
Axes of the slice: x: 4, y: 8, z: 16, core: 2. Of those that a mesh axis runs over, the one named last changes fastest.
Arguments:
- act_send: bfloat16 [8192, 3584], P(('section', 'expert')), may hold values from -6 to 6
- grad_send: bfloat16 [8192, 3584], P(('section', 'expert')), may hold values from -6 to 6
- x_back: bfloat16 [8192, 3584], P(('section', 'expert')), may hold values from -6 to 6
- routes_fwd: int32 [8192, 2], P(('section', 'expert')), may hold values from 0 to 7, all different within a row; in each aligned block of 8 rows (0 to 7, 8 to 15, ...) at most 4 rows name the same one
- gates_fwd: float32 [8192, 2], P(('section', 'expert')), may hold values from 0.3 to 1
- routes_back: int32 [8192, 2], P(('section', 'expert')), may hold values from 0 to 7, all different within a row; in each aligned block of 8 rows (0 to 7, 8 to 15, ...) at most 4 rows name the same one
- gates_back: float32 [8192, 2], P(('section', 'expert')), may hold values from 0.3 to 1
- norm_gain: float32 [16, 3584], P('section'), may hold values from 0.5 to 1.5
- w_gate: bfloat16 [16, 64, 3584, 128], P('section', 'expert'), may hold values from -0.09375 to 0.09375
- w_up: bfloat16 [16, 64, 3584, 128], P('section', 'expert'), may hold values from -0.09375 to 0.09375
- w_down: bfloat16 [16, 64, 128, 3584], P('section', 'expert'), may hold values from -0.1875 to 0.1875
- stash: bfloat16 [16, 64, 64, 4, 256], P('section', 'expert'), may hold values from -6 to 6
Outputs:
- outbound: bfloat16 [8192, 3584], P(('section', 'expert'))
- input_grad: bfloat16 [8192, 3584], P(('section', 'expert'))
Inputs may be any that keep to these rules, and one draw needn't show every extreme that they name: `routes_fwd`: each row names 2 different experts; among the rows of one device no expert is named more than 4 times, a bound that some block reaches. `routes_back`: each row names 2 different experts; among the rows of one device no expert is named more than 4 times, a bound that some block reaches.
All inputs are finite; a program needn't handle non-finite values.
Results may differ from a plain program's by a relative error of at most 0.0055.
Values may be sent and summed in bfloat16 or wider, within the bound.
A program may use at most 32 MiB of HBM per device.

v0:
```python
import jax
import jax.numpy as jnp
from jax import lax
from jax.sharding import PartitionSpec as P

EPSILON = 1e-06
HIGHEST = lax.Precision.HIGHEST


def from_behind(value, axis, by):
    size = lax.axis_size(axis)
    return lax.ppermute(value, axis, [(i, (i + by) % size) for i in range(size)])


def slot_tables(routes, gates, experts, capacity):
    tokens_here = routes.shape[0]
    chosen = routes.reshape(-1)
    onehot = (chosen[:, None] == jnp.arange(experts, dtype=jnp.int32)[None, :]).astype(jnp.int32)
    earlier = jnp.cumsum(onehot, axis=0) - onehot
    within = jnp.sum(earlier * onehot, axis=1)
    target = chosen * capacity + within
    slot_table = (
        target[:, None] == jnp.arange(experts * capacity, dtype=jnp.int32)[None, :]
    ).astype(jnp.float32)
    slot_table = slot_table.reshape(tokens_here, routes.shape[1], experts * capacity)
    occupancy = jnp.sum(slot_table, axis=1).T
    weighted = jnp.sum(slot_table * gates[:, :, None], axis=1)
    return (occupancy, weighted)


def normalize(values, scale_row):
    factor = lax.rsqrt(jnp.mean(values * values, axis=-1, keepdims=True) + EPSILON)
    return (values * factor * scale_row, factor)


def fan_out(slot_rows, groups, shards):
    capacity = slot_rows.shape[0] // groups
    columns = slot_rows.shape[1]
    spread = jnp.broadcast_to(
        slot_rows.reshape(groups, 1, capacity, columns), (groups, shards, capacity, columns)
    )
    return spread.reshape(groups * shards, capacity, columns)


def return_sums(partial_value, groups, shards):
    sources, capacity, columns = partial_value.shape
    arrived = lax.all_to_all(partial_value, "expert", split_axis=0, concat_axis=0, tiled=True)
    summed = arrived.reshape(groups, shards, capacity, columns).astype(jnp.float32).sum(axis=1)
    return summed.reshape(groups * capacity, columns)


def body(
    act_send,
    grad_send,
    x_back,
    routes_fwd,
    gates_fwd,
    routes_back,
    gates_back,
    norm_gain,
    w_gate,
    w_up,
    w_down,
    stash,
):
    sources = lax.axis_size("expert")
    shards = min(8, sources // 2)
    groups = sources // shards
    capacity = stash.shape[3]
    hidden_dev = w_gate.shape[3]
    columns = act_send.shape[1]
    scale_row = norm_gain[0]
    gate_weight = w_gate[0, 0]
    up_weight = w_up[0, 0]
    down_weight = w_down[0, 0]
    inbound = from_behind(act_send, "section", 1)
    cotangent = from_behind(grad_send, "section", -1)
    normed = normalize(inbound.astype(jnp.float32), scale_row)[0].astype(jnp.bfloat16)
    occupancy_fwd, weighted_fwd = slot_tables(routes_fwd, gates_fwd, groups, capacity)
    slot_rows = jnp.dot(
        occupancy_fwd.astype(jnp.bfloat16), normed, preferred_element_type=jnp.float32
    ).astype(jnp.bfloat16)
    received = lax.all_to_all(
        fan_out(slot_rows, groups, shards), "expert", split_axis=0, concat_axis=0, tiled=True
    )
    flat_rows = received.reshape(-1, columns)
    gate_pre = jnp.dot(flat_rows, gate_weight, preferred_element_type=jnp.float32)
    up_pre = jnp.dot(flat_rows, up_weight, preferred_element_type=jnp.float32)
    hidden = (jax.nn.silu(gate_pre) * up_pre).astype(jnp.bfloat16)
    partial_value = jnp.dot(hidden, down_weight, preferred_element_type=jnp.float32).astype(
        jnp.bfloat16
    )
    summed = return_sums(partial_value.reshape(sources, capacity, columns), groups, shards)
    mixture = jnp.dot(weighted_fwd, summed, precision=HIGHEST)
    outbound = (inbound.astype(jnp.float32) + mixture).astype(jnp.bfloat16)
    occupancy_back, weighted_back = slot_tables(routes_back, gates_back, groups, capacity)
    grad_rows = jnp.dot(weighted_back.T, cotangent.astype(jnp.float32), precision=HIGHEST).astype(
        jnp.bfloat16
    )
    grad_received = lax.all_to_all(
        fan_out(grad_rows, groups, shards), "expert", split_axis=0, concat_axis=0, tiled=True
    )
    grad_flat = grad_received.reshape(-1, columns)
    saved_pre = stash[0, 0].reshape(-1, 2 * hidden_dev).astype(jnp.float32)
    saved_gate = saved_pre[:, :hidden_dev]
    saved_up = saved_pre[:, hidden_dev:]
    grad_hidden = jnp.einsum(
        "rd,hd->rh", grad_flat, down_weight, preferred_element_type=jnp.float32
    )
    sigmoid = jax.nn.sigmoid(saved_gate)
    d_gate = (grad_hidden * saved_up * sigmoid * (1.0 + saved_gate * (1.0 - sigmoid))).astype(
        jnp.bfloat16
    )
    d_up = (grad_hidden * saved_gate * sigmoid).astype(jnp.bfloat16)
    grad_total = jnp.einsum("rh,dh->rd", d_gate, gate_weight, preferred_element_type=jnp.float32)
    grad_total = grad_total + jnp.einsum(
        "rh,dh->rd", d_up, up_weight, preferred_element_type=jnp.float32
    )
    grad_partial = grad_total.astype(jnp.bfloat16)
    grad_summed = return_sums(grad_partial.reshape(sources, capacity, columns), groups, shards)
    grad_normed = jnp.dot(occupancy_back.T, grad_summed, precision=HIGHEST)
    saved32 = x_back.astype(jnp.float32)
    factor = normalize(saved32, scale_row)[1]
    scaled_grad = grad_normed * scale_row
    through = factor * scaled_grad - saved32 * factor**3 * jnp.mean(
        scaled_grad * saved32, axis=-1, keepdims=True
    )
    input_grad = (cotangent.astype(jnp.float32) + through).astype(jnp.bfloat16)
    return (outbound, input_grad)


def solution(mesh):
    placed = (
        P(("section", "expert"), None),
        P(("section", "expert"), None),
        P(("section", "expert"), None),
        P(("section", "expert"), None),
        P(("section", "expert"), None),
        P(("section", "expert"), None),
        P(("section", "expert"), None),
        P("section", None),
        P("section", "expert", None, None),
        P("section", "expert", None, None),
        P("section", "expert", None, None),
        P("section", "expert", None, None, None),
    )
    return jax.shard_map(
        body,
        mesh=mesh,
        in_specs=placed,
        out_specs=(P(("section", "expert"), None), P(("section", "expert"), None)),
        check_vma=False,
    )
```

profile of v0, /device:TPU:56, one launch (start us, length us, event | category | flops | bytes accessed | tf_op | source)
XLA Modules:
  0.0 406.1 jit_solution(12581384661846764544)
XLA Ops:
  0.6 0.8 collective-permute-start.1
  1.4 0.8 copy.29
  2.2 0.1 eq.65
  2.3 0.1 fusion.37
  2.4 0.2 select_reduce_fusion.1
  2.6 0.1 reduce_sum.111
  2.7 0.1 copy.31
  2.8 0.8 select_reduce_fusion
  3.5 0.1 collective-permute-done.1
  3.6 0.4 convolution_convert_fusion.1
  4.0 0.1 broadcast_in_dim.10
  4.0 1.7 broadcast_in_dim.11
  5.8 22.4 %all-to-all-start.2 = ((bf16[64,4,3584]{2,1,0:T(4,128)(2,1)}), bf16[64,4,3584]{2,1,0:T(4,128)(2,1)S(1)}, u32[]{:S(2)}, u32[]{:S(2)}) async-start(bf16[64,4,3584]{2,1,0:T(4,128)(2,1)} %bitcast.34), calls=%async_computation.2 | async-start | bytes 3670016 | tf_op jit(solution)/shard_map/all_to_all | solution.py:100
  28.2 1.7 collective-permute-start
  29.8 0.1 copy.26
  29.9 0.1 eq.58
  30.0 0.1 fusion.38
  30.1 0.2 select_reduce_fusion.3
  30.3 0.1 reduce_sum.104
  30.4 0.1 copy.28
  30.5 0.1 convert_reduce_fusion.3
  30.6 1.2 collective-permute-done
  31.8 0.1 fusion.21
  31.9 0.3 convolution_convert_fusion.2
  32.3 82.9 %all-to-all-done.2 = bf16[64,4,3584]{2,1,0:T(4,128)(2,1)S(1)} async-done(((bf16[64,4,3584]{2,1,0:T(4,128)(2,1)}), bf16[64,4,3584]{2,1,0:T(4,128)(2,1)S(1)}, u32[]{:S(2)}, u32[]{:S(2)}) %all-to-all-start.2) | async-done | bytes 1835040 | tf_op jit(solution)/shard_map/all_to_all | solution.py:100
  115.2 1.7 broadcast_in_dim.9
  116.9 8.8 %all-to-all-start = ((bf16[64,4,3584]{2,1,0:T(4,128)(2,1)}), bf16[64,4,3584]{2,1,0:T(4,128)(2,1)}, u32[]{:S(2)}, u32[]{:S(2)}) async-start(bf16[64,4,3584]{2,1,0:T(4,128)(2,1)} %bitcast.35), calls=%async_computation | async-start | bytes 3670016 | tf_op jit(solution)/shard_map/all_to_all | solution.py:83
  125.8 1.5 reshape.111
  127.3 2.4 fusion.3
  129.7 0.6 fusion.9
  130.4 0.7 fusion
  131.0 1.5 reshape.112
  132.5 82.9 %all-to-all-done = bf16[64,4,3584]{2,1,0:T(4,128)(2,1)} async-done(((bf16[64,4,3584]{2,1,0:T(4,128)(2,1)}), bf16[64,4,3584]{2,1,0:T(4,128)(2,1)}, u32[]{:S(2)}, u32[]{:S(2)}) %all-to-all-start) | async-done | bytes 1835040 | tf_op jit(solution)/shard_map/all_to_all | solution.py:83
  215.4 6.1 %all-to-all-start.3 = ((bf16[64,4,3584]{2,1,0:T(4,128)(2,1)}), bf16[64,4,3584]{2,1,0:T(4,128)(2,1)}, u32[]{:S(2)}, u32[]{:S(2)}) async-start(bf16[64,4,3584]{2,1,0:T(4,128)(2,1)} %reshape.112), calls=%async_computation.3 | async-start | bytes 3670016 | tf_op jit(solution)/shard_map/all_to_all | solution.py:47
  221.4 2.9 reshape.107
  224.4 1.8 fusion.11
  226.2 3.7 convolution_convert_fusion
  229.9 4.1 %reshape.108 = bf16[64,4,3584]{2,1,0:T(4,128)(2,1)} reshape(bf16[256,3584]{1,0:T(8,128)(2,1)} %convolution_convert_fusion) | data formatting | bytes 3670016 | tf_op jit(solution)/shard_map/reshape | solution.py:93
  233.9 75.9 %all-to-all-done.3 = bf16[64,4,3584]{2,1,0:T(4,128)(2,1)} async-done(((bf16[64,4,3584]{2,1,0:T(4,128)(2,1)}), bf16[64,4,3584]{2,1,0:T(4,128)(2,1)}, u32[]{:S(2)}, u32[]{:S(2)}) %all-to-all-start.3) | async-done | bytes 1835040 | tf_op jit(solution)/shard_map/all_to_all | solution.py:47
  309.8 6.0 %all-to-all-start.1 = ((bf16[64,4,3584]{2,1,0:T(4,128)(2,1)}), bf16[64,4,3584]{2,1,0:T(4,128)(2,1)S(1)}, u32[]{:S(2)}, u32[]{:S(2)}) async-start(bf16[64,4,3584]{2,1,0:T(4,128)(2,1)} %reshape.108), calls=%async_computation.1 | async-start | bytes 3670016 | tf_op jit(solution)/shard_map/all_to_all | solution.py:47
  315.9 3.2 convert_reduce_fusion
  319.0 1.2 reshape.113
  320.2 0.5 fusion.24
  320.7 82.8 %all-to-all-done.1 = bf16[64,4,3584]{2,1,0:T(4,128)(2,1)S(1)} async-done(((bf16[64,4,3584]{2,1,0:T(4,128)(2,1)}), bf16[64,4,3584]{2,1,0:T(4,128)(2,1)S(1)}, u32[]{:S(2)}, u32[]{:S(2)}) %all-to-all-start.1) | async-done | bytes 1835040 | tf_op jit(solution)/shard_map/all_to_all | solution.py:47
  403.5 0.8 convert_reduce_fusion.1
  404.3 0.2 reshape.109
  404.4 1.0 fusion.1
  405.4 0.7 fusion.28
  (26 shorter events, 0.3 us)
Async XLA Ops:
  0.6 129.7 %copy-start = (bf16[1,1,3584,128]{3,2,1,0:T(8,128)(2,1)S(1)}, bf16[1,1,3584,128]{3,2,1,0:T(8,128)(2,1)}, u32[]{:S(2)}) copy-start(bf16[1,1,3584,128]{3,2,1,0:T(8,128)(2,1)} %param.21) | copy-start | bytes 2752516
  0.6 2.9 collective-permute-start.1
  5.8 22.4 %copy-start.7 = (bf16[8,3584]{1,0:T(8,128)(2,1)S(1)}, bf16[8,3584]{1,0:T(8,128)(2,1)}, u32[]{:S(2)}) copy-start(bf16[8,3584]{1,0:T(8,128)(2,1)} %param.12) | copy-start | bytes 172036
  5.8 24.1 %copy-start.5 = (s32[8,2]{0,1:T(2,128)S(1)}, s32[8,2]{0,1:T(2,128)}, u32[]{:S(2)}) copy-start(s32[8,2]{0,1:T(2,128)} %param.15) | copy-start | bytes 196
  5.8 24.7 %copy-start.6 = (f32[8,2]{0,1:T(2,128)S(1)}, f32[8,2]{0,1:T(2,128)}, u32[]{:S(2)}) copy-start(f32[8,2]{0,1:T(2,128)} %param.16) | copy-start | bytes 196
  5.8 24.8 %copy-start.4 = (f32[1,3584]{1,0:T(1,128)S(1)}, f32[1,3584]{1,0:T(1,128)}, u32[]{:S(2)}) copy-start(f32[1,3584]{1,0:T(1,128)} %param.19) | copy-start | bytes 43012
  5.8 109.4 %all-to-all-start.2 = ((bf16[64,4,3584]{2,1,0:T(4,128)(2,1)}), bf16[64,4,3584]{2,1,0:T(4,128)(2,1)S(1)}, u32[]{:S(2)}, u32[]{:S(2)}) async-start(bf16[64,4,3584]{2,1,0:T(4,128)(2,1)} %bitcast.34), calls=%async_computation.2 | async-start | bytes 3670016 | tf_op jit(solution)/shard_map/all_to_all | solution.py:100
  28.2 3.6 collective-permute-start
  116.9 8.8 %copy-start.3 = (bf16[1,1,64,4,256]{4,3,2,1,0:T(4,128)(2,1)S(1)}, bf16[1,1,64,4,256]{4,3,2,1,0:T(4,128)(2,1)}, u32[]{:S(2)}) copy-start(bf16[1,1,64,4,256]{4,3,2,1,0:T(4,128)(2,1)} %param.23) | copy-start | bytes 393220
  116.9 98.4 %all-to-all-start = ((bf16[64,4,3584]{2,1,0:T(4,128)(2,1)}), bf16[64,4,3584]{2,1,0:T(4,128)(2,1)}, u32[]{:S(2)}, u32[]{:S(2)}) async-start(bf16[64,4,3584]{2,1,0:T(4,128)(2,1)} %bitcast.35), calls=%async_computation | async-start | bytes 3670016 | tf_op jit(solution)/shard_map/all_to_all | solution.py:83
  127.3 2.4 copy-start.1
  215.4 94.5 %all-to-all-start.3 = ((bf16[64,4,3584]{2,1,0:T(4,128)(2,1)}), bf16[64,4,3584]{2,1,0:T(4,128)(2,1)}, u32[]{:S(2)}, u32[]{:S(2)}) async-start(bf16[64,4,3584]{2,1,0:T(4,128)(2,1)} %reshape.112), calls=%async_computation.3 | async-start | bytes 3670016 | tf_op jit(solution)/shard_map/all_to_all | solution.py:47
  309.8 93.6 %all-to-all-start.1 = ((bf16[64,4,3584]{2,1,0:T(4,128)(2,1)}), bf16[64,4,3584]{2,1,0:T(4,128)(2,1)S(1)}, u32[]{:S(2)}, u32[]{:S(2)}) async-start(bf16[64,4,3584]{2,1,0:T(4,128)(2,1)} %reshape.108), calls=%async_computation.1 | async-start | bytes 3670016 | tf_op jit(solution)/shard_map/all_to_all | solution.py:47
  315.9 4.4 %copy-start.2 = (bf16[8,3584]{1,0:T(8,128)(2,1)S(1)}, bf16[8,3584]{1,0:T(8,128)(2,1)}, u32[]{:S(2)}) copy-start(bf16[8,3584]{1,0:T(8,128)(2,1)} %param.14) | copy-start | bytes 172036
where the time goes:
time: 407 us; the launch traced here: 406 us
  waiting for transfers between devices  326 us (80%)
  starting transfers between devices  45.7 us (11%)
  local copies, waits for them, and re-layouts  16.2 us (4%)
  matrix products  11.3 us (3%)
  other arithmetic  6.32 us (2%)
    all_to_all x2, waiting for transfers between devices, return_sums(): lax.all_to_all(partial_value, 'expert', split_axis=0, concat_axis=0, tile...  159 us
    all_to_all x1, waiting for transfers between devices, body(): lax.all_to_all(fan_out(grad_rows, groups, shards), 'expert', split_axis=0...  82.9 us
    all_to_all x1, waiting for transfers between devices, body(): lax.all_to_all(fan_out(slot_rows, groups, shards), 'expert', split_axis=0...  82.9 us
    all_to_all x1, starting transfers between devices, body(): lax.all_to_all(fan_out(grad_rows, groups, shards), 'expert', split_axis=0...  22.4 us
    all_to_all x2, starting transfers between devices, return_sums(): lax.all_to_all(partial_value, 'expert', split_axis=0, concat_axis=0, tile...  12.1 us
    all_to_all x1, starting transfers between devices, body(): lax.all_to_all(fan_out(slot_rows, groups, shards), 'expert', split_axis=0...  8.81 us
  transfers between devices with their start and end apart: 6, of which 6 were waited for; matrix products, arithmetic and copies ran while one was open for 7% of the time, Pallas kernels for 0%

commit v1 on v0

v1 whole, which is shorter than its diff:
```python
import functools

import jax
import jax.numpy as jnp
from jax import lax
from jax.experimental import pallas as pl
from jax.experimental.pallas import tpu as pltpu
from jax.sharding import PartitionSpec as P

EPSILON = 1e-06
HIGHEST = lax.Precision.HIGHEST
MESH = pl.DeviceIdType.MESH
F32 = jnp.float32
BF16 = jnp.bfloat16

PLANES = 16
COLS = 4
STEPS = 8
EXPERTS = 8
CAP = 4


def kernel(
    act, grad, x_back, routes_fwd, gates_fwd, routes_back, gates_back, gain, w_gate, w_up, w_down, stash,
    outbound, input_grad,
    wgu, wdn, inb, cot, slots, xb, hid, ob, ra, rb, fl, fr, keep, ps, pr, ts, fb,
    shift_send, shift_recv, load_sem, send, zr, pr_in, lr, rr, fa, fbs, ra_in, rb_in, fl_in, fr_in, pb_in, fin,
):
    width = act.shape[1]
    half = width // 2
    quarter = half // 2
    n_section = lax.axis_size("section")
    s = lax.axis_index("section")
    me = lax.axis_index("expert")
    z = me // COLS
    x = lax.rem(me, COLS)
    parity = lax.rem(z, 2)
    sg = 2 * parity - 1
    mine = z // 2

    def plane(v):
        return lax.rem(v + 2 * PLANES, PLANES)

    def at_plane(v):
        return {"expert": plane(v) * COLS + x}

    right = {"expert": z * COLS + lax.rem(x + 1, COLS)}
    left = {"expert": z * COLS + lax.rem(x + COLS - 1, COLS)}
    partner = at_plane(z - sg)
    after = {"section": lax.rem(s + 1, n_section)}
    before = {"section": lax.rem(s + n_section - 1, n_section)}

    def remote(src, dst, send_sem, recv_sem, device):
        pltpu.make_async_remote_copy(
            src_ref=src, dst_ref=dst, send_sem=send_sem, recv_sem=recv_sem, device_id=device, device_id_type=MESH
        ).start()

    def arrive(ref, sem):
        pltpu.make_async_copy(ref, ref, sem).wait()

    loads = [
        pltpu.make_async_copy(w_gate, wgu.at[:, 0:128], load_sem.at[0]),
        pltpu.make_async_copy(w_up, wgu.at[:, 128:256], load_sem.at[1]),
        pltpu.make_async_copy(w_down, wdn, load_sem.at[2]),
    ]
    for load in loads:
        load.start()

    barrier = pltpu.get_barrier_semaphore()
    everyone = [after, before, left, right, partner]
    everyone += [at_plane(z + sg * d) for d in range(1, STEPS)]
    everyone += [at_plane(z - sg * 2 * k) for k in range(1, STEPS // 2)]
    for device in everyone:
        pl.semaphore_signal(barrier, inc=1, device_id=device, device_id_type=MESH)
    pl.semaphore_wait(barrier, len(everyone))

    remote(act, inb, shift_send.at[0], shift_recv.at[0], after)
    remote(grad, cot, shift_send.at[1], shift_recv.at[1], before)

    def tables(routes_ref, gates_ref):
        lane = lax.broadcasted_iota(jnp.int32, (8, 64), 1)
        expert = lane >> 3
        rank = (lane & 3).astype(F32)
        m0 = jnp.where(routes_ref[:, 0:1] == expert, 1.0, 0.0)
        m1 = jnp.where(routes_ref[:, 1:2] == expert, 1.0, 0.0)
        m = m0 + m1
        lower = jnp.where(
            lax.broadcasted_iota(jnp.int32, (8, 8), 0) > lax.broadcasted_iota(jnp.int32, (8, 8), 1), 1.0, 0.0
        )
        earlier = jnp.dot(lower, m, preferred_element_type=F32, precision=HIGHEST)
        here = jnp.where(earlier == rank, m, 0.0)
        weighted = jnp.where(here > 0.0, m0 * gates_ref[:, 0:1] + m1 * gates_ref[:, 1:2], 0.0)
        return here, weighted

    here_f, weight_f = tables(routes_fwd, gates_fwd)
    here_b, weight_b = tables(routes_back, gates_back)
    top_lane = (lax.broadcasted_iota(jnp.int32, (8, 64), 1) & 4) == 0

    def row_top(rows):
        return (lax.broadcasted_iota(jnp.int32, (rows, 1), 0) & 4) == 0

    def pick(table, values, precision):
        dims = (((0,), (0,)), ((), ()))
        a = lax.dot_general(table, values[:, :half], dims, preferred_element_type=F32, precision=precision)
        b = lax.dot_general(table, values[:, half:], dims, preferred_element_type=F32, precision=precision)
        return jnp.where(row_top(64), a, b).astype(BF16).reshape(EXPERTS, 8, half)

    def send_slots(f):
        for k in range(STEPS // 2):
            same = plane(z - sg * 2 * k)
            if k == 0:
                pltpu.make_async_copy(slots.at[f, mine], xb.at[f, 0, 0, 0], zr.at[f, 0]).start()
            else:
                remote(slots.at[f, same // 2], xb.at[f, 0, 2 * k, 0], send.at[f, 0], zr.at[f, 2 * k], at_plane(same))
            other = plane(z + sg * (2 * k + 1))
            remote(
                slots.at[f, other // 2], xb.at[f, 0, 2 * k + 1, 0], send.at[f, 0], zr.at[f, 2 * k + 1], at_plane(other)
            )

    arrive(inb, shift_recv.at[0])
    inbound = inb[...].astype(F32)
    factor = lax.rsqrt(jnp.mean(inbound * inbound, axis=-1, keepdims=True) + EPSILON)
    normed = (inbound * factor * gain[...]).astype(BF16)
    slots[0] = pick(here_f.astype(BF16), normed, None)
    send_slots(0)
    arrive(cot, shift_recv.at[1])
    slots[1] = pick(weight_b, cot[...].astype(F32), HIGHEST)
    send_slots(1)

    def to_partner(f, d):
        arrive(xb.at[f, 0, d, 0], zr.at[f, d])
        remote(xb.at[f, 0, d, 0], xb.at[f, 0, d, 1], send.at[f, 1], pr_in.at[f, d], partner)

    def to_sides(f, d):
        arrive(xb.at[f, 0, d, 1], pr_in.at[f, d])
        remote(xb.at[f, 0, d], xb.at[f, 1, d], send.at[f, 2], lr.at[f, d], right)
        remote(xb.at[f, 0, d], xb.at[f, 2, d], send.at[f, 3], rr.at[f, d], left)

    def to_far(f, d):
        arrive(xb.at[f, 1, d], lr.at[f, d])
        remote(
            xb.at[f, 1, d, :, :, 0:quarter], xb.at[f, 3, d, :, :, 0:quarter], send.at[f, 4], fa.at[f, d], right
        )
        arrive(xb.at[f, 2, d], rr.at[f, d])
        remote(
            xb.at[f, 2, d, :, :, quarter:half], xb.at[f, 3, d, :, :, quarter:half], send.at[f, 5], fbs.at[f, d], left
        )

    def dispatch_step(f, j):
        @pl.when(j < STEPS)
        def _():
            to_partner(f, j)

        @pl.when(jnp.logical_and(j >= 1, j < STEPS + 1))
        def _():
            to_sides(f, j - 1)

        @pl.when(j >= 3)
        def _():
            to_far(f, j - 3)

    def far_arrived(f):
        @pl.loop(0, STEPS)
        def _(d):
            arrive(xb.at[f, 3, d, :, :, 0:quarter], fa.at[f, d])
            arrive(xb.at[f, 3, d, :, :, quarter:half], fbs.at[f, d])

    ROWS = STEPS * 2 * 8
    top = row_top(ROWS)

    def both_halves(a, b):
        v = jnp.where(top, a, b)
        return v + jnp.where(top, pltpu.roll(v, ROWS - 4, 0), pltpu.roll(v, 4, 0))

    def rows_of(f, rel):
        return xb[f, rel].astype(F32).reshape(ROWS, half).astype(BF16)

    def forward_hidden(rel):
        rows = rows_of(0, rel)
        a = jnp.dot(rows, wgu[0:half, :], preferred_element_type=F32)
        b = jnp.dot(rows, wgu[half:width, :], preferred_element_type=F32)
        v = both_halves(a, b)
        gate, up = v[:, :128], v[:, 128:]
        hid[rel] = (gate / (1.0 + jnp.exp(-gate)) * up).astype(BF16)

    def forward_out(rel):
        h = hid[rel]
        a = jnp.dot(h, wdn[:, 0:half], preferred_element_type=F32)
        b = jnp.dot(h, wdn[:, half:width], preferred_element_type=F32)
        ob[0, rel] = jnp.where(top, a, b).reshape(STEPS, 2, 8, half).astype(BF16)

    NT = (((1,), (1,)), ((), ()))

    def backward(rel):
        rows = rows_of(1, rel)
        a = lax.dot_general(rows, wdn[:, 0:half], NT, preferred_element_type=F32)
        b = lax.dot_general(rows, wdn[:, half:width], NT, preferred_element_type=F32)
        dh = both_halves(a, b)
        col = lax.rem(x + jnp.where(rel == 1, 3, jnp.where(rel == 2, 1, jnp.where(rel == 3, 2, 0))), COLS)
        saved = []
        for d in range(STEPS):
            for zs in (plane(z + sg * d), plane(z - sg * (1 + d))):
                saved.append(stash[zs * COLS + col].astype(F32))
        saved = jnp.concatenate(saved, axis=0)
        gate, up = saved[:, :128], saved[:, 128:]
        sig = 1.0 / (1.0 + jnp.exp(-gate))
        d_gate = dh * up * sig * (1.0 + gate * (1.0 - sig))
        d_up = dh * gate * sig
        d_both = jnp.concatenate([d_gate, d_up], axis=1).astype(BF16)
        a = lax.dot_general(d_both, wgu[0:half, :], NT, preferred_element_type=F32)
        b = lax.dot_general(d_both, wgu[half:width, :], NT, preferred_element_type=F32)
        ob[1, rel] = jnp.where(top, a, b).reshape(STEPS, 2, 8, half).astype(BF16)

    def far_out(f):
        @pl.loop(0, STEPS)
        def _(j):
            d = STEPS - 1 - j
            remote(ob.at[f, 3, d, :, :, 0:quarter], ra.at[f, d], send.at[f, 6], ra_in.at[f, d], left)
            remote(ob.at[f, 3, d, :, :, quarter:half], rb.at[f, d], send.at[f, 7], rb_in.at[f, d], right)

    def sides_out(f, d):
        arrive(ra.at[f, d], ra_in.at[f, d])
        v = ob[f, 1, d, :, :, 0:quarter].astype(F32) + ra[f, d].astype(F32)
        ob[f, 1, d, :, :, 0:quarter] = v.astype(BF16)
        remote(ob.at[f, 1, d], fr.at[f, d], send.at[f, 8], fr_in.at[f, d], left)
        arrive(rb.at[f, d], rb_in.at[f, d])
        v = ob[f, 2, d, :, :, quarter:half].astype(F32) + rb[f, d].astype(F32)
        ob[f, 2, d, :, :, quarter:half] = v.astype(BF16)
        remote(ob.at[f, 2, d], fl.at[f, d], send.at[f, 9], fl_in.at[f, d], right)

    def pair_out(f, d):
        arrive(fr.at[f, d], fr_in.at[f, d])
        arrive(fl.at[f, d], fl_in.at[f, d])
        v = ob[f, 0, d].astype(F32) + fr[f, d].astype(F32) + fl[f, d].astype(F32)
        keep[f, d] = v[0]
        ps[f, d] = v[1].astype(BF16)
        remote(ps.at[f, d], pr.at[f, d], send.at[f, 10], pb_in.at[f, d], partner)

    def source_out(f, d):
        arrive(pr.at[f, d], pb_in.at[f, d])
        ts[f, d] = (keep[f, d] + pr[f, d].astype(F32)).astype(BF16)

        @pl.when(d == 0)
        def _():
            pltpu.make_async_copy(ts.at[f, d], fb.at[f, mine], fin.at[f, mine]).start()

        @pl.when(d > 0)
        def _():
            remote(ts.at[f, d], fb.at[f, mine], send.at[f, 11], fin.at[f, mine], at_plane(z + sg * d))

    def gathered(f, table):
        for e in range(EXPERTS):
            arrive(fb.at[f, e], fin.at[f, e])
        rows = fb[f].astype(F32).reshape(EXPERTS * 8, half)
        a = jnp.dot(jnp.where(top_lane, table, 0.0), rows, preferred_element_type=F32, precision=HIGHEST)
        b = jnp.dot(jnp.where(top_lane, 0.0, table), rows, preferred_element_type=F32, precision=HIGHEST)
        return jnp.concatenate([a, b], axis=1)

    @pl.loop(0, STEPS + 3)
    def _(j):
        dispatch_step(0, j)

    for load in loads:
        load.wait()

    @pl.loop(0, STEPS + 3)
    def _(j):
        dispatch_step(1, j)

        @pl.when(jnp.logical_and(lax.rem(j, 2) == 0, jnp.logical_and(j >= 2, j < 10)))
        def _():
            rel = (j - 2) // 2

            @pl.when(rel == 3)
            def _():
                far_arrived(0)

            forward_hidden(rel)

    @pl.loop(0, COLS)
    def _(j):
        rel = COLS - 1 - j
        forward_out(rel)

        @pl.when(j == 0)
        def _():
            far_out(0)

    far_arrived(1)

    @pl.loop(0, COLS)
    def _(j):
        rel = COLS - 1 - j
        backward(rel)

        @pl.when(j == 0)
        def _():
            far_out(1)

        sides_out(0, STEPS - 1 - 2 * j)
        sides_out(0, STEPS - 2 - 2 * j)

    @pl.loop(0, STEPS + 1)
    def _(j):
        @pl.when(j < STEPS)
        def _():
            sides_out(1, STEPS - 1 - j)
            pair_out(0, STEPS - 1 - j)

        @pl.when(j >= 1)
        def _():
            source_out(0, STEPS - j)

    @pl.loop(0, STEPS + 1)
    def _(j):
        @pl.when(j < STEPS)
        def _():
            pair_out(1, STEPS - 1 - j)

        @pl.when(j >= 1)
        def _():
            source_out(1, STEPS - j)

    outbound[...] = (inb[...].astype(F32) + gathered(0, weight_f)).astype(BF16)

    grad_normed = gathered(1, here_b)
    saved = x_back[...].astype(F32)
    factor_b = lax.rsqrt(jnp.mean(saved * saved, axis=-1, keepdims=True) + EPSILON)
    scaled = grad_normed * gain[...]
    through = factor_b * scaled - saved * (factor_b * factor_b * factor_b) * jnp.mean(
        scaled * saved, axis=-1, keepdims=True
    )
    input_grad[...] = (cot[...].astype(F32) + through).astype(BF16)

    arrive(act, shift_send.at[0])
    arrive(grad, shift_send.at[1])
    for f in range(2):
        arrive(xb.at[f, 0, 1:8, 0], send.at[f, 0])
        arrive(xb.at[f, 0, :, 0], send.at[f, 1])
        arrive(xb.at[f, 0], send.at[f, 2])
        arrive(xb.at[f, 0], send.at[f, 3])
        arrive(xb.at[f, 1, :, :, :, 0:quarter], send.at[f, 4])
        arrive(xb.at[f, 2, :, :, :, quarter:half], send.at[f, 5])
        arrive(ra.at[f], send.at[f, 6])
        arrive(rb.at[f], send.at[f, 7])
        arrive(ob.at[f, 1], send.at[f, 8])
        arrive(ob.at[f, 2], send.at[f, 9])
        arrive(ps.at[f], send.at[f, 10])
        arrive(ts.at[f, 1:8], send.at[f, 11])


def body(
    act_send, grad_send, x_back, routes_fwd, gates_fwd, routes_back, gates_back, norm_gain, w_gate, w_up, w_down, stash
):
    rows, width = act_send.shape
    half = width // 2
    any_space = pl.BlockSpec(memory_space=pl.ANY)
    vmem = pl.BlockSpec(memory_space=pltpu.VMEM)
    twice = jnp.concatenate([stash[0, 0], stash[0, 0]], axis=1)
    dma = pltpu.SemaphoreType.DMA
    return pl.pallas_call(
        kernel,
        out_shape=(
            jax.ShapeDtypeStruct((rows, width), BF16),
            jax.ShapeDtypeStruct((rows, width), BF16),
        ),
        in_specs=[any_space, any_space] + [vmem] * 6 + [any_space] * 3 + [vmem],
        out_specs=(vmem, vmem),
        scratch_shapes=[
            pltpu.VMEM((width, 256), BF16),
            pltpu.VMEM((128, width), BF16),
            pltpu.VMEM((rows, width), BF16),
            pltpu.VMEM((rows, width), BF16),
            pltpu.VMEM((2, EXPERTS, 8, half), BF16),
            pltpu.VMEM((2, COLS, STEPS, 2, 8, half), BF16),
            pltpu.VMEM((COLS, STEPS * 16, 128), BF16),
            pltpu.VMEM((2, COLS, STEPS, 2, 8, half), BF16),
            pltpu.VMEM((2, STEPS, 2, 8, half // 2), BF16),
            pltpu.VMEM((2, STEPS, 2, 8, half // 2), BF16),
            pltpu.VMEM((2, STEPS, 2, 8, half), BF16),
            pltpu.VMEM((2, STEPS, 2, 8, half), BF16),
            pltpu.VMEM((2, STEPS, 8, half), F32),
            pltpu.VMEM((2, STEPS, 8, half), BF16),
            pltpu.VMEM((2, STEPS, 8, half), BF16),
            pltpu.VMEM((2, STEPS, 8, half), BF16),
            pltpu.VMEM((2, EXPERTS, 8, half), BF16),
            dma((2,)),
            dma((2,)),
            dma((3,)),
            dma((2, 12)),
        ]
        + [dma((2, STEPS))] * 12,
        compiler_params=pltpu.CompilerParams(
            collective_id=0, has_side_effects=True, vmem_limit_bytes=48 * 1024 * 1024
        ),
    )(
        act_send, grad_send, x_back, routes_fwd, gates_fwd, routes_back, gates_back, norm_gain,
        w_gate[0, 0], w_up[0, 0], w_down[0, 0], twice,
    )


def solution(mesh):
    rows = P(("section", "expert"), None)
    held = P("section", "expert", None, None)
    return jax.shard_map(
        body,
        mesh=mesh,
        in_specs=(rows,) * 7 + (P("section", None), held, held, held, P("section", "expert", None, None, None)),
        out_specs=(rows, rows),
        check_vma=False,
    )
```

time: 407 us -> 134 us (0.33)
  waiting for transfers between devices: 326 us -> 0 us
  Pallas kernels: 0 us -> 123 us
  starting transfers between devices: 45.7 us -> 0 us
  matrix products: 11.3 us -> 0 us
  local copies, waits for them, and re-layouts: 16.2 us -> 7.58 us
  other arithmetic: 6.32 us -> 1.11 us
    all_to_all x4 -> x0, waiting for transfers between devices: 324 us -> none  [the longest x2 159 us: return_sums(): lax.all_to_all(partial_value, 'expert', split_axis=0, concat_axis=0, tile...]
    pallas_call x0 -> x1, Pallas kernels: none -> 123 us  [body(): pl.pallas_call(kernel, out_shape=(jax.ShapeDtypeStruct((rows, width), BF1...]
    all_to_all x4 -> x0, starting transfers between devices: 43.3 us -> none  [the longest x1 22.4 us: body(): lax.all_to_all(fan_out(grad_rows, groups, shards), 'expert', split_axis=0...]
    dot_general x9 -> x0, matrix products: 11.3 us -> none  [the longest x1 3.65 us: body(): jnp.dot(hidden, down_weight, preferred_element_type=jnp.float32)]
    reshape x6 -> x0, local copies, waits for them, and re-layouts: 11.3 us -> none  [the longest x1 4.07 us: body(): partial_value.reshape(sources, capacity, columns)]
    unnamed x18 -> x28, local copies, waits for them, and re-layouts: 0.87 us -> 7.58 us
    reduce_sum x7 -> x0, other arithmetic: 5.3 us -> none  [the longest x2 3.95 us: return_sums(): arrived.reshape(groups, shards, capacity, columns).astype(jnp.float32)]
  transfers between devices with their start and end apart: 6 -> 0, of which waited for: 6 -> 0; matrix products, arithmetic and copies ran while one was open for 7% -> 0% of each run, Pallas kernels for 0% -> 0%
where the time goes in v1:
time: 134 us; the launch traced here: 133 us
  Pallas kernels  123 us (92%)
  local copies, waits for them, and re-layouts  7.58 us (6%)
    pallas_call x1, Pallas kernels, body(): pl.pallas_call(kernel, out_shape=(jax.ShapeDtypeStruct((rows, width), BF1...  123 us
    unnamed x28, local copies, waits for them, and re-layouts  7.58 us

profile of v1, /device:TPU:56, one launch (start us, length us, event | category | flops | bytes accessed | tf_op | source)
XLA Modules:
  0.0 132.8 jit_solution(11760537960964603253)
XLA Ops:
  0.6 0.0 copy-start.7
  0.6 0.7 copy-done.7
  1.3 0.0 copy-start.8
  1.3 0.1 copy.14.routes_fwd
  1.4 0.6 copy-done.8
  2.0 0.0 copy-start.9
  2.0 0.1 copy.15.gates_fwd
  2.1 0.6 copy-done.9
  2.7 0.0 copy-start.10
  2.7 0.1 copy.16.routes_back
  2.8 0.6 copy-done.10
  3.3 0.1 copy.17.gates_back
  3.4 0.0 copy-start.3
  3.4 0.0 copy-start.4
  3.4 0.0 copy-start.5
  3.4 0.0 copy-start.6
  3.4 1.1 pad_maximum_fusion.stash
  4.6 0.0 copy-done.3
  4.6 0.0 copy-done.4
  4.6 0.0 copy-done.5
  4.6 0.0 copy-done.6
  4.6 0.0 copy-start
  4.6 1.2 copy-done
  5.8 0.0 copy-start.1
  5.8 1.2 copy-done.1
  7.0 0.0 copy-start.2
  7.0 1.2 copy-done.2
  8.1 123.4 %shard_map.131 = (bf16[8,3584]{1,0:T(8,128)(2,1)S(1)}, bf16[8,3584]{1,0:T(8,128)(2,1)S(1)}) custom-call(bf16[8,3584]{1,0:T(8,128)(2,1)S(1)} %copy-done.3, bf16[8,3584]{1,0:T(8,128)(2,1)S(1)} %copy-done.4, bf16[8,3584]{1,0:T(8,128)(2,1)S(1)} %copy-done.5, s32[8,2]{1,0:T(8,128)S(1)} %copy.14.routes_fwd, f32[8,2]{1,0:T(8,128)S(1)} %copy.15.gates_fwd, ...), custom_call_target="tpu_custom_call" | custom-call | tf_op jit(solution)/shard_map/pallas_call | solution.py:361
  131.5 0.6 copy.20
  132.1 0.6 copy.21
Async XLA Ops:
  0.6 0.7 copy-start.7
  1.3 0.7 copy-start.8
  2.0 0.7 copy-start.9
  2.7 0.7 copy-start.10
  3.4 1.1 copy-start.3
  3.4 1.1 copy-start.4
  3.4 1.1 copy-start.5
  3.4 1.1 copy-start.6
  4.6 1.2 copy-start
  5.8 1.2 copy-start.1
  7.0 1.2 copy-start.2

commit v2 on v1

v2 whole, which is shorter than its diff:
```python
import functools

import jax
import jax.numpy as jnp
from jax import lax
from jax.experimental import pallas as pl
from jax.experimental.pallas import tpu as pltpu
from jax.sharding import PartitionSpec as P

EPSILON = 1e-06
HIGHEST = lax.Precision.HIGHEST
MESH = pl.DeviceIdType.MESH
F32 = jnp.float32
BF16 = jnp.bfloat16

PLANES = 16
COLS = 4
STEPS = 8
EXPERTS = 8
CAP = 4
AHEAD = 6
LAGS = (0, 1, 3, 6, 8, 11, 13)


def kernel(
    act, grad, x_back_in, routes_fwd_in, gates_fwd_in, routes_back_in, gates_back_in, gain_in, w_gate, w_up, w_down,
    stash_in,
    outbound, input_grad,
    x_back, routes_fwd, gates_fwd, routes_back, gates_back, gain, stash, wgu, wdn, inb, cot, slots, xb, ob, ra, rb, fl, fr, keep, ps, pr, ts, fb,
    shift_send, shift_recv, load_sem, send, zr, pr_in, lr, rr, fa, fbs, ra_in, rb_in, fl_in, fr_in, pb_in, fin,
):
    width = act.shape[1]
    half = width // 2
    quarter = half // 2
    n_section = lax.axis_size("section")
    s = lax.axis_index("section")
    me = lax.axis_index("expert")
    z = me // COLS
    x = lax.rem(me, COLS)
    parity = lax.rem(z, 2)
    sg = 2 * parity - 1
    mine = z // 2

    def plane(v):
        return lax.rem(v + 2 * PLANES, PLANES)

    def at_plane(v):
        return {"expert": plane(v) * COLS + x}

    right = {"expert": z * COLS + lax.rem(x + 1, COLS)}
    left = {"expert": z * COLS + lax.rem(x + COLS - 1, COLS)}
    partner = at_plane(z - sg)
    after = {"section": lax.rem(s + 1, n_section)}
    before = {"section": lax.rem(s + n_section - 1, n_section)}

    def remote(src, dst, send_sem, recv_sem, device):
        pltpu.make_async_remote_copy(
            src_ref=src, dst_ref=dst, send_sem=send_sem, recv_sem=recv_sem, device_id=device, device_id_type=MESH
        ).start()

    def arrive(ref, sem):
        pltpu.make_async_copy(ref, ref, sem).wait()

    pairs = [
        (routes_fwd_in, routes_fwd), (gates_fwd_in, gates_fwd), (routes_back_in, routes_back),
        (gates_back_in, gates_back), (gain_in, gain), (x_back_in, x_back), (stash_in, stash),
        (w_gate, wgu.at[:, 0:128]), (w_up, wgu.at[:, 128:256]), (w_down, wdn),
    ]
    loads = [pltpu.make_async_copy(src, dst, load_sem.at[i]) for i, (src, dst) in enumerate(pairs)]
    early, late = loads[:5], loads[5:]
    for load in early:
        load.start()

    barrier = pltpu.get_barrier_semaphore()
    everyone = [after, before, left, right, partner]
    everyone += [at_plane(z + sg * d) for d in range(1, STEPS)]
    everyone += [at_plane(z - sg * 2 * k) for k in range(1, STEPS // 2)]
    for device in everyone:
        pl.semaphore_signal(barrier, inc=1, device_id=device, device_id_type=MESH)
    pl.semaphore_wait(barrier, len(everyone))

    remote(act, inb, shift_send.at[0], shift_recv.at[0], after)
    remote(grad, cot, shift_send.at[1], shift_recv.at[1], before)
    for load in late:
        load.start()
    for load in early:
        load.wait()

    def tables(routes_ref, gates_ref):
        row = lax.broadcasted_iota(jnp.int32, (64, 8), 0)
        expert = row >> 3
        rank = (row & 3).astype(F32)
        m0 = jnp.where(routes_ref[0:1, :] == expert, 1.0, 0.0)
        m1 = jnp.where(routes_ref[1:2, :] == expert, 1.0, 0.0)
        m = m0 + m1
        before_it = jnp.where(
            lax.broadcasted_iota(jnp.int32, (8, 8), 0) < lax.broadcasted_iota(jnp.int32, (8, 8), 1), 1.0, 0.0
        )
        earlier = jnp.dot(m.astype(BF16), before_it.astype(BF16), preferred_element_type=F32)
        here = jnp.where(earlier == rank, m, 0.0)
        weighted = jnp.where(here > 0.0, m0 * gates_ref[0:1, :] + m1 * gates_ref[1:2, :], 0.0)
        return here, weighted

    here_f, weight_f = tables(routes_fwd, gates_fwd)
    here_b, weight_b = tables(routes_back, gates_back)

    def row_top(rows):
        return (lax.broadcasted_iota(jnp.int32, (rows, 1), 0) & 4) == 0

    def pick(table, values):
        chosen = table.astype(BF16)
        a = jnp.dot(chosen, values[:, :half], preferred_element_type=F32)
        b = jnp.dot(chosen, values[:, half:], preferred_element_type=F32)
        return jnp.where(row_top(64), a, b)

    def put_slots(f, rows):
        slots[f] = rows.astype(BF16).reshape(EXPERTS, 8, half)

    def send_own(f):
        remote(slots.at[f, mine], xb.at[f, 0, 0, 1], send.at[f, 1], pr_in.at[f, 0], partner)
        pltpu.make_async_copy(slots.at[f, mine], xb.at[f, 0, 0, 0], zr.at[f, 0]).start()

    def send_slots(f, d):
        there = plane(z + sg * (2 * lax.rem(d, 2) - 1) * d)
        remote(slots.at[f, there // 2], xb.at[f, 0, d, 0], send.at[f, 0], zr.at[f, d], at_plane(there))

    def prepare(f):
        if f == 0:
            arrive(inb, shift_recv.at[0])
            inbound = inb[...].astype(F32)
            factor = lax.rsqrt(jnp.mean(inbound * inbound, axis=-1, keepdims=True) + EPSILON)
            put_slots(0, pick(here_f, (inbound * factor * gain[...]).astype(BF16)))
        else:
            arrive(cot, shift_recv.at[1])
            put_slots(1, pick(here_b, cot[...]) * jnp.sum(weight_b, axis=1, keepdims=True))

    def either(f, work):
        @pl.when(f == 0)
        def _():
            work(0)

        @pl.when(f == 1)
        def _():
            work(1)

    first = lax.rem(s + 1, 2)
    second = 1 - first
    either(first, prepare)
    send_own(first)
    either(second, prepare)
    send_own(second)

    def to_partner(f, d):
        arrive(xb.at[f, 0, d, 0], zr.at[f, d])

        @pl.when(d > 0)
        def _():
            remote(xb.at[f, 0, d, 0], xb.at[f, 0, d, 1], send.at[f, 1], pr_in.at[f, d], partner)

    def to_sides(f, d):
        arrive(xb.at[f, 0, d, 1], pr_in.at[f, d])
        remote(xb.at[f, 0, d], xb.at[f, 1, d], send.at[f, 2], lr.at[f, d], right)
        remote(xb.at[f, 0, d], xb.at[f, 2, d], send.at[f, 3], rr.at[f, d], left)

    def to_far(f, d):
        arrive(xb.at[f, 1, d], lr.at[f, d])
        remote(
            xb.at[f, 1, d, :, :, 0:quarter], xb.at[f, 3, d, :, :, 0:quarter], send.at[f, 4], fa.at[f, d], right
        )
        arrive(xb.at[f, 2, d], rr.at[f, d])
        remote(
            xb.at[f, 2, d, :, :, quarter:half], xb.at[f, 3, d, :, :, quarter:half], send.at[f, 5], fbs.at[f, d], left
        )

    ROWS = COLS * 2 * 8
    top = row_top(ROWS)

    def both_halves(a, b):
        v = jnp.where(top, a, b)
        return v + jnp.where(top, pltpu.roll(v, ROWS - 4, 0), pltpu.roll(v, 4, 0))

    def rows_of(f, d):
        return xb[f, :, d].astype(F32).reshape(ROWS, half).astype(BF16)

    def forward(d):
        rows = rows_of(0, d)
        a = jnp.dot(rows, wgu[0:half, :], preferred_element_type=F32)
        b = jnp.dot(rows, wgu[half:width, :], preferred_element_type=F32)
        v = both_halves(a, b)
        gate, up = v[:, :128], v[:, 128:]
        h = (gate / (1.0 + jnp.exp(-gate)) * up).astype(BF16)
        a = jnp.dot(h, wdn[:, 0:half], preferred_element_type=F32)
        b = jnp.dot(h, wdn[:, half:width], preferred_element_type=F32)
        ob[0, :, d] = jnp.where(top, a, b).reshape(COLS, 2, 8, half).astype(BF16)

    NT = (((1,), (1,)), ((), ()))

    def backward(d):
        rows = rows_of(1, d)
        a = lax.dot_general(rows, wdn[:, 0:half], NT, preferred_element_type=F32)
        b = lax.dot_general(rows, wdn[:, half:width], NT, preferred_element_type=F32)
        dh = both_halves(a, b)
        saved = []
        for step in (0, 3, 1, 2):
            col = lax.rem(x + step, COLS)
            for zs in (plane(z + sg * d), plane(z - sg * (1 + d))):
                own = stash[zs * COLS + col].astype(F32)
                saved += [own, own]
        saved = jnp.concatenate(saved, axis=0)
        gate, up = saved[:, :128], saved[:, 128:]
        sig = 1.0 / (1.0 + jnp.exp(-gate))
        d_gate = dh * up * sig * (1.0 + gate * (1.0 - sig))
        d_up = dh * gate * sig
        d_both = jnp.concatenate([d_gate, d_up], axis=1).astype(BF16)
        a = lax.dot_general(d_both, wgu[0:half, :], NT, preferred_element_type=F32)
        b = lax.dot_general(d_both, wgu[half:width, :], NT, preferred_element_type=F32)
        ob[1, :, d] = jnp.where(top, a, b).reshape(COLS, 2, 8, half).astype(BF16)

    def far_out(f, d):
        remote(ob.at[f, 3, d, :, :, 0:quarter], ra.at[f, d], send.at[f, 6], ra_in.at[f, d], left)
        remote(ob.at[f, 3, d, :, :, quarter:half], rb.at[f, d], send.at[f, 7], rb_in.at[f, d], right)

    def sides_out(f, d):
        arrive(ra.at[f, d], ra_in.at[f, d])
        v = ob[f, 1, d, :, :, 0:quarter].astype(F32) + ra[f, d].astype(F32)
        ob[f, 1, d, :, :, 0:quarter] = v.astype(BF16)
        remote(ob.at[f, 1, d], fr.at[f, d], send.at[f, 8], fr_in.at[f, d], left)
        arrive(rb.at[f, d], rb_in.at[f, d])
        v = ob[f, 2, d, :, :, quarter:half].astype(F32) + rb[f, d].astype(F32)
        ob[f, 2, d, :, :, quarter:half] = v.astype(BF16)
        remote(ob.at[f, 2, d], fl.at[f, d], send.at[f, 9], fl_in.at[f, d], right)

    def pair_out(f, d):
        arrive(fr.at[f, d], fr_in.at[f, d])
        arrive(fl.at[f, d], fl_in.at[f, d])
        v = ob[f, 0, d].astype(F32) + fr[f, d].astype(F32) + fl[f, d].astype(F32)
        keep[f, d] = v[0]
        ps[f, d] = v[1].astype(BF16)
        remote(ps.at[f, d], pr.at[f, d], send.at[f, 10], pb_in.at[f, d], partner)

    def source_out(f, d):
        arrive(pr.at[f, d], pb_in.at[f, d])
        ts[f, d] = (keep[f, d] + pr[f, d].astype(F32)).astype(BF16)

        @pl.when(d == 0)
        def _():
            pltpu.make_async_copy(ts.at[f, d], fb.at[f, mine], fin.at[f, mine]).start()

        @pl.when(d > 0)
        def _():
            remote(ts.at[f, d], fb.at[f, mine], send.at[f, 11], fin.at[f, mine], at_plane(z + sg * d))

    def gathered(f, parts):
        for e in range(EXPERTS):
            arrive(fb.at[f, e], fin.at[f, e])
        rows = fb[f].astype(F32).reshape(EXPERTS * 8, half).astype(BF16)
        dims = (((0,), (0,)), ((), ()))
        both = []
        for kept in (row_top(64), jnp.logical_not(row_top(64))):
            terms = [
                lax.dot_general(jnp.where(kept, t, 0.0).astype(BF16), rows, dims, preferred_element_type=F32)
                for t in parts
            ]
            both.append(functools.reduce(jnp.add, terms))
        return jnp.concatenate(both, axis=1)

    def compute(f, d):
        arrive(xb.at[f, 3, d, :, :, 0:quarter], fa.at[f, d])
        arrive(xb.at[f, 3, d, :, :, quarter:half], fbs.at[f, d])
        either(f, lambda which: (forward, backward)[which](d))
        far_out(f, d)

    def unit(v, work):
        work(lax.rem(first + v, 2), lax.rem(STEPS - v // 2, STEPS))

    @pl.loop(2, AHEAD)
    def _(v):
        unit(v, send_slots)

    for load in late:
        load.wait()

    stages = (to_partner, to_sides, to_far, compute, sides_out, pair_out, source_out)

    @pl.loop(0, 2 * STEPS + max(LAGS))
    def _(u):
        @pl.when(u + AHEAD < 2 * STEPS)
        def _():
            unit(u + AHEAD, send_slots)

        for lag, stage in zip(LAGS, stages):
            @pl.when(jnp.logical_and(u >= lag, u < 2 * STEPS + lag))
            def _(lag=lag, stage=stage):
                unit(u - lag, stage)

    high = weight_f.astype(BF16).astype(F32)
    middle = (weight_f - high).astype(BF16).astype(F32)
    weight_parts = [high, middle, weight_f - high - middle]
    outbound[...] = (inb[...].astype(F32) + gathered(0, weight_parts)).astype(BF16)

    grad_normed = gathered(1, [here_b])
    saved = x_back[...].astype(F32)
    factor_b = lax.rsqrt(jnp.mean(saved * saved, axis=-1, keepdims=True) + EPSILON)
    scaled = grad_normed * gain[...]
    through = factor_b * scaled - saved * (factor_b * factor_b * factor_b) * jnp.mean(
        scaled * saved, axis=-1, keepdims=True
    )
    input_grad[...] = (cot[...].astype(F32) + through).astype(BF16)

    arrive(act, shift_send.at[0])
    arrive(grad, shift_send.at[1])
    for f in range(2):
        arrive(xb.at[f, 0, 1:8, 0], send.at[f, 0])
        arrive(xb.at[f, 0, :, 0], send.at[f, 1])
        arrive(xb.at[f, 0], send.at[f, 2])
        arrive(xb.at[f, 0], send.at[f, 3])
        arrive(xb.at[f, 1, :, :, :, 0:quarter], send.at[f, 4])
        arrive(xb.at[f, 2, :, :, :, quarter:half], send.at[f, 5])
        arrive(ra.at[f], send.at[f, 6])
        arrive(rb.at[f], send.at[f, 7])
        arrive(ob.at[f, 1], send.at[f, 8])
        arrive(ob.at[f, 2], send.at[f, 9])
        arrive(ps.at[f], send.at[f, 10])
        arrive(ts.at[f, 1:8], send.at[f, 11])


def body(
    act_send, grad_send, x_back, routes_fwd, gates_fwd, routes_back, gates_back, norm_gain, w_gate, w_up, w_down, stash
):
    rows, width = act_send.shape
    half = width // 2
    hbm = pl.BlockSpec(memory_space=pltpu.HBM)
    vmem = pl.BlockSpec(memory_space=pltpu.VMEM)
    dma = pltpu.SemaphoreType.DMA
    return pl.pallas_call(
        kernel,
        out_shape=(
            jax.ShapeDtypeStruct((rows, width), BF16),
            jax.ShapeDtypeStruct((rows, width), BF16),
        ),
        in_specs=[hbm] * 12,
        out_specs=(vmem, vmem),
        scratch_shapes=[
            pltpu.VMEM((rows, width), BF16),
            pltpu.VMEM((2, rows), jnp.int32),
            pltpu.VMEM((2, rows), F32),
            pltpu.VMEM((2, rows), jnp.int32),
            pltpu.VMEM((2, rows), F32),
            pltpu.VMEM((1, width), F32),
            pltpu.VMEM(stash.shape[2:], BF16),
            pltpu.VMEM((width, 256), BF16),
            pltpu.VMEM((128, width), BF16),
            pltpu.VMEM((rows, width), BF16),
            pltpu.VMEM((rows, width), BF16),
            pltpu.VMEM((2, EXPERTS, 8, half), BF16),
            pltpu.VMEM((2, COLS, STEPS, 2, 8, half), BF16),
            pltpu.VMEM((2, COLS, STEPS, 2, 8, half), BF16),
            pltpu.VMEM((2, STEPS, 2, 8, half // 2), BF16),
            pltpu.VMEM((2, STEPS, 2, 8, half // 2), BF16),
            pltpu.VMEM((2, STEPS, 2, 8, half), BF16),
            pltpu.VMEM((2, STEPS, 2, 8, half), BF16),
            pltpu.VMEM((2, STEPS, 8, half), F32),
            pltpu.VMEM((2, STEPS, 8, half), BF16),
            pltpu.VMEM((2, STEPS, 8, half), BF16),
            pltpu.VMEM((2, STEPS, 8, half), BF16),
            pltpu.VMEM((2, EXPERTS, 8, half), BF16),
            dma((2,)),
            dma((2,)),
            dma((10,)),
            dma((2, 12)),
        ]
        + [dma((2, STEPS))] * 12,
        compiler_params=pltpu.CompilerParams(
            collective_id=0, has_side_effects=True, vmem_limit_bytes=67043328
        ),
    )(
        act_send, grad_send, x_back, routes_fwd.T, gates_fwd.T, routes_back.T, gates_back.T, norm_gain,
        w_gate[0, 0], w_up[0, 0], w_down[0, 0], stash[0, 0],
    )


def solution(mesh):
    rows = P(("section", "expert"), None)
    held = P("section", "expert", None, None)
    return jax.shard_map(
        body,
        mesh=mesh,
        in_specs=(rows,) * 7 + (P("section", None), held, held, held, P("section", "expert", None, None, None)),
        out_specs=(rows, rows),
        check_vma=False,
    )
```

time: 134 us -> 116 us (0.87)
  Pallas kernels: 123 us -> 111 us
  local copies, waits for them, and re-layouts: 7.58 us -> 2.09 us
    pallas_call x1, Pallas kernels: 123 us -> 111 us  [body(): pl.pallas_call(kernel, out_shape=(jax.ShapeDtypeStruct((rows, width), BF1...]
    unnamed x28 -> x4, local copies, waits for them, and re-layouts: 7.58 us -> 2.09 us
where the time goes in v2:
time: 116 us; the launch traced here: 114 us
  Pallas kernels  111 us (96%)
  local copies, waits for them, and re-layouts  2.09 us (2%)
    pallas_call x1, Pallas kernels, body(): pl.pallas_call(kernel, out_shape=(jax.ShapeDtypeStruct((rows, width), BF1...  111 us

profile of v2, /device:TPU:56, one launch (start us, length us, event | category | flops | bytes accessed | tf_op | source)
XLA Modules:
  0.0 114.0 jit_solution(1608805396813380712)
XLA Ops:
  0.6 111.3 %shard_map.131 = (bf16[8,3584]{1,0:T(8,128)(2,1)}, bf16[8,3584]{1,0:T(8,128)(2,1)}) custom-call(bf16[8,3584]{1,0:T(8,128)(2,1)} %act.1, bf16[8,3584]{1,0:T(8,128)(2,1)} %grad.1, bf16[8,3584]{1,0:T(8,128)(2,1)} %x_back_in.1, s32[2,8]{1,0:T(2,128)} %bitcast.12, f32[2,8]{1,0:T(2,128)} %bitcast.13, s32[2,8]{1,0:T(2,128)} %bitcast.14, f32[2,8]{1,0:T(2,128)} %bitcast.15, ...), custom_call_target="tpu_custom_call" | custom-call | tf_op jit(solution)/shard_map/pallas_call | solution.py:335
  111.9 0.0 copy-start
  111.9 1.5 %copy.16 = bf16[8,3584]{1,0:T(8,128)(2,1)} copy(bf16[8,3584]{1,0:T(8,128)(2,1)} %get-tuple-element.4) | data formatting | bytes 114688
  113.4 0.0 copy-done
  113.4 0.6 copy.17
Async XLA Ops:
  111.9 1.5 %copy-start = (bf16[8,3584]{1,0:T(8,128)(2,1)S(1)}, bf16[8,3584]{1,0:T(8,128)(2,1)}, u32[]{:S(2)}) copy-start(bf16[8,3584]{1,0:T(8,128)(2,1)} %get-tuple-element.5) | copy-start | bytes 172036
